TPU v7x, 32 devices: a whole 2x2x4 slice. The times are simulated.
32 devices in a mesh: ord: 8 (over z, core), gx: 2 (over x), gy: 2 (over y).
Axes of the slice: x: 2, y: 2, z: 4, core: 2. Of those that a mesh axis runs over, the one named last changes fastest.
Arguments:
- distribution: float32 [256, 64, 8, 128], P('ord', 'gx', 'gy'), may hold values from -4.5 to 4.5
- relaxation: float32 [64, 8, 128], P('gx', 'gy'), may hold values from 0.05 to 5
Outputs:
- updated: float32 [256, 64, 8, 128], P('ord', 'gx', 'gy')
- temperature: float32 [64, 8, 128], P('gx', 'gy')
All inputs are finite; a program needn't handle non-finite values.
Results may differ from a plain program's by a relative error of at most 0.0003.
Values sent between devices are 32-bit elements; how exact they have to be, the bound alone decides.
A program may use at most 64 MiB of HBM per device.

v0:
```python
import jax
import jax.numpy as jnp
from jax import lax
from jax.sharding import PartitionSpec as P

NORD = 256
STEPS = 2
SWEEPS = 3


time_step = 0.4
limiter_eps = 0.01
diffusion_mass = 0.5
flux_weight = 2.0
golden_turn = 2.399963229728653


def extended(cells, sides, width):
    for axis, dim in sides:
        count = lax.axis_size(axis)
        ends = count - 1
        head = lax.slice_in_dim(cells, 0, width, axis=dim)
        tail = lax.slice_in_dim(cells, cells.shape[dim] - width, cells.shape[dim], axis=dim)
        cells = jnp.concatenate(
            [
                lax.ppermute(tail, axis, [(i, (i + 1) % count) for i in range(ends)]),
                cells,
                lax.ppermute(head, axis, [((i + 1) % count, i) for i in range(ends)]),
            ],
            axis=dim,
        )
    return cells


def directions(offset, length):
    ordinal = (offset + jnp.arange(length, dtype=jnp.int32)).astype(jnp.float32)
    height = 1.0 - (2.0 * ordinal + 1.0) / NORD
    radius = jnp.sqrt(1.0 - height * height)
    turned = golden_turn * ordinal
    return jnp.stack([radius * jnp.cos(turned), radius * jnp.sin(turned), height])


def window(values, anchor, length, axis_dim):
    return lax.slice_in_dim(values, anchor, anchor + length, axis=axis_dim)


def pad_along(values, width, axis_dim):
    widths = [
        (width, width) if dimension == axis_dim else (0, 0) for dimension in range(values.ndim)
    ]
    return jnp.pad(values, widths)


def source_of(current, local_temp, relax):
    return ((2.0 * relax - time_step) * current + 2.0 * time_step * local_temp) / (
        2.0 * relax + time_step
    )


def axis_flux(padded, temp_pad, relax_pad, along_speed, axis_dim):
    length = padded.shape[axis_dim] - 4
    lower_diff = window(padded, 1, length + 2, axis_dim) - window(padded, 0, length + 2, axis_dim)
    upper_diff = window(padded, 2, length + 2, axis_dim) - window(padded, 1, length + 2, axis_dim)
    centre = window(padded, 1, length + 2, axis_dim)
    slopes = (
        lower_diff * (upper_diff * upper_diff + limiter_eps)
        + upper_diff * (lower_diff * lower_diff + limiter_eps)
    ) / (lower_diff * lower_diff + upper_diff * upper_diff + 2.0 * limiter_eps)
    upwind_low = window(centre, 0, length + 1, axis_dim) + 0.5 * (
        1.0 - time_step * along_speed
    ) * window(slopes, 0, length + 1, axis_dim)
    upwind_high = window(centre, 1, length + 1, axis_dim) - 0.5 * (
        1.0 + time_step * along_speed
    ) * window(slopes, 1, length + 1, axis_dim)
    upwind = jnp.where(along_speed >= 0.0, upwind_low, upwind_high)
    temp_face = 0.5 * (
        window(temp_pad, 0, length + 1, axis_dim) + window(temp_pad, 1, length + 1, axis_dim)
    )
    relax_face = 0.5 * (
        window(relax_pad, 0, length + 1, axis_dim) + window(relax_pad, 1, length + 1, axis_dim)
    )
    edges = (2.0 * relax_face * upwind + 0.5 * time_step * temp_face) / (
        2.0 * relax_face + 0.5 * time_step
    )
    return along_speed * (window(edges, 1, length, axis_dim) - window(edges, 0, length, axis_dim))


def spread(flux_x_pad, flux_y_pad, flux_z):
    flux_z_pad = jnp.pad(flux_z, ((0, 0), (0, 0), (1, 1)))
    result = 0.5 * (flux_x_pad[2:, 1:-1, 1:-1] - flux_x_pad[:-2, 1:-1, 1:-1])
    result = result + 0.5 * (flux_y_pad[1:-1, 2:, 1:-1] - flux_y_pad[1:-1, :-2, 1:-1])
    return result + 0.5 * (flux_z_pad[:, :, 2:] - flux_z_pad[:, :, :-2])


def relax_sweep(potential_pad, driver):
    conduct = 1.0 / (1.0 + potential_pad * potential_pad)
    centre = conduct[1:-1, 1:-1, 1:-1]
    weighted = diffusion_mass * driver
    weights = diffusion_mass + jnp.zeros_like(driver)
    for axis_dim in range(3):
        for anchor in (0, 2):
            picker = tuple(
                (
                    (
                        slice(anchor, anchor + potential_pad.shape[axis_dim] - 2)
                        if dimension == axis_dim
                        else slice(1, -1)
                    )
                    for dimension in range(3)
                )
            )
            couple = 0.5 * (centre + conduct[picker])
            weighted = weighted + couple * potential_pad[picker]
            weights = weights + couple
    return weighted / weights


def transport(current, local_temp, relax, speeds):
    source = source_of(current, local_temp, relax)
    ordinal_rows = source.shape[0]
    stacked = jnp.concatenate([source, local_temp[None], relax[None]], 0)
    widened = extended(stacked, (("gx", 1), ("gy", 2)), 2)
    along_x = widened[:, :, 2:-2, :]
    along_y = widened[:, 2:-2, :, :]
    fluxes = axis_flux(
        along_x[:ordinal_rows],
        along_x[ordinal_rows : ordinal_rows + 1, 1:-1],
        along_x[ordinal_rows + 1 :, 1:-1],
        speeds[0][:, None, None, None],
        1,
    )
    fluxes = fluxes + axis_flux(
        along_y[:ordinal_rows],
        along_y[ordinal_rows : ordinal_rows + 1, :, 1:-1],
        along_y[ordinal_rows + 1 :, :, 1:-1],
        speeds[1][:, None, None, None],
        2,
    )
    fluxes = fluxes + axis_flux(
        pad_along(source, 2, 3),
        pad_along(local_temp[None], 1, 3),
        pad_along(relax[None], 1, 3),
        speeds[2][:, None, None, None],
        3,
    )
    return source - time_step * fluxes


def block_extend(stacked):
    widened = extended(stacked, (("gx", 1), ("gy", 2)), 1)
    return jnp.pad(widened, ((0, 0), (0, 0), (0, 0), (1, 1)))


def diffuse(shares, extend):
    energy = shares[0]
    widened = extend(shares[:3])
    driver = energy - flux_weight * spread(widened[1], widened[2], shares[3])
    potential = relax_sweep(widened[0], driver)
    for rounds in range(1, SWEEPS):
        potential = relax_sweep(extend(potential[None])[0], driver)
    return potential


def local(distribution, relaxation):
    local_count = distribution.shape[0]
    speeds = directions(lax.axis_index("ord") * local_count, local_count)
    current = distribution
    for repeat in range(STEPS):
        local_temp = lax.psum(jnp.sum(current, 0) / NORD, "ord")
        current = transport(current, local_temp, relaxation, speeds)
    partial_value = (
        jnp.concatenate(
            [jnp.sum(current, 0)[None], jnp.sum(speeds[:, :, None, None, None] * current[None], 1)],
            0,
        )
        / NORD
    )
    shares = lax.psum(partial_value, "ord")
    potential = diffuse(shares, block_extend)
    updated = source_of(current, potential, relaxation)
    return (updated, potential)


def solution(mesh):
    placed = (P("ord", "gx", "gy", None), P("gx", "gy", None))
    return jax.shard_map(
        local,
        mesh=mesh,
        in_specs=placed,
        out_specs=(P("ord", "gx", "gy", None), P("gx", "gy", None)),
        check_vma=False,
    )
```

profile of v0, /device:TPU:0, one launch (start us, length us, event | category | flops | bytes accessed | tf_op | source)
XLA Modules:
  0.0 365.7 jit_solution(15019233585724942882)
XLA Ops:
  12.2 56.1 %all-reduce.13.cloned.1.call-done = f32[32,4,128]{2,1,0:T(4,128)} async-done(((f32[32,4,128]{2,1,0:T(4,128)}), f32[32,4,128]{2,1,0:T(4,128)}) %all-reduce.13.cloned.1.call-update) | async-done | bytes 65552 | tf_op jit(solution)/shard_map/psum | solution.py:169
  74.3 3.4 collective-permute-start
  85.2 3.5 collective-permute-start.2
  93.6 21.6 %collective-permute-done.2 = f32[34,36,2,128]{3,1,2,0:T(8,128)S(1)} collective-permute-done((f32[34,36,2,128]{3,1,2,0:T(8,128)S(1)}, f32[34,36,2,128]{3,1,2,0:T(8,128)S(1)}, u32[]{:S(2)}, u32[]{:S(2)}) %collective-permute-start.2) | collective-permute-done | bytes 1253408 | tf_op jit(solution)/shard_map/ppermute | solution.py:26
  115.3 4.2 %collective-permute-done.3 = f32[34,36,2,128]{3,1,2,0:T(8,128)S(1)} collective-permute-done((f32[34,36,2,128]{3,1,2,0:T(8,128)S(1)}, f32[34,36,2,128]{3,1,2,0:T(8,128)S(1)}, u32[]{:S(2)}, u32[]{:S(2)}) %collective-permute-start.3) | collective-permute-done | bytes 1253408 | tf_op jit(solution)/shard_map/ppermute | solution.py:28
  119.5 3.6 fusion.18
  123.1 3.5 add_divide_fusion.3
  131.0 53.0 %all-reduce.15.cloned.1.call-done = f32[32,4,128]{2,1,0:T(4,128)} async-done(((f32[32,4,128]{2,1,0:T(4,128)}), f32[32,4,128]{2,1,0:T(4,128)}) %all-reduce.15.cloned.1.call-update) | async-done | bytes 65552 | tf_op jit(solution)/shard_map/psum | solution.py:169
  189.8 3.4 collective-permute-start.4
  200.8 3.5 collective-permute-start.6
  209.1 21.8 %collective-permute-done.6 = f32[34,36,2,128]{3,1,2,0:T(8,128)S(1)} collective-permute-done((f32[34,36,2,128]{3,1,2,0:T(8,128)S(1)}, f32[34,36,2,128]{3,1,2,0:T(8,128)S(1)}, u32[]{:S(2)}, u32[]{:S(2)}) %collective-permute-start.6) | collective-permute-done | bytes 1253408 | tf_op jit(solution)/shard_map/ppermute | solution.py:26
  230.9 4.2 %collective-permute-done.7 = f32[34,36,2,128]{3,1,2,0:T(8,128)S(1)} collective-permute-done((f32[34,36,2,128]{3,1,2,0:T(8,128)S(1)}, f32[34,36,2,128]{3,1,2,0:T(8,128)S(1)}, u32[]{:S(2)}, u32[]{:S(2)}) %collective-permute-start.7) | collective-permute-done | bytes 1253408 | tf_op jit(solution)/shard_map/ppermute | solution.py:28
  235.1 3.6 fusion.21
  238.7 3.5 add_divide_fusion.2
  248.7 53.9 %all-reduce.17.cloned.1.call-done = f32[4,32,4,128]{3,2,1,0:T(4,128)} async-done(((f32[4,32,4,128]{3,2,1,0:T(4,128)}), f32[4,32,4,128]{3,2,1,0:T(4,128)}) %all-reduce.17.cloned.1.call-update) | async-done | bytes 262160 | tf_op jit(solution)/shard_map/psum | solution.py:178
  303.2 3.4 collective-permute-start.8
  308.9 3.3 collective-permute-done.9
  312.2 3.4 collective-permute-start.10
  318.0 3.6 collective-permute-done.11
  327.1 4.2 %collective-permute-done.13 = f32[1,1,4,128]{3,2,1,0:T(4,128)S(1)} collective-permute-done((f32[1,1,4,128]{3,2,1,0:T(4,128)S(1)}, f32[1,1,4,128]{3,2,1,0:T(4,128)S(1)}, u32[]{:S(2)}, u32[]{:S(2)}) %collective-permute-start.13) | collective-permute-done | bytes 2080 | tf_op jit(solution)/shard_map/ppermute | solution.py:28
  334.3 4.2 %collective-permute-done.15 = f32[1,34,1,128]{3,2,1,0:T(1,128)S(1)} collective-permute-done((f32[1,34,1,128]{3,2,1,0:T(1,128)S(1)}, f32[1,34,1,128]{3,2,1,0:T(1,128)S(1)}, u32[]{:S(2)}, u32[]{:S(2)}) %collective-permute-start.15) | collective-permute-done | bytes 17440 | tf_op jit(solution)/shard_map/ppermute | solution.py:28
  342.6 4.2 %collective-permute-done.17 = f32[1,1,4,128]{3,2,1,0:T(4,128)S(1)} collective-permute-done((f32[1,1,4,128]{3,2,1,0:T(4,128)S(1)}, f32[1,1,4,128]{3,2,1,0:T(4,128)S(1)}, u32[]{:S(2)}, u32[]{:S(2)}) %collective-permute-start.17) | collective-permute-done | bytes 2080 | tf_op jit(solution)/shard_map/ppermute | solution.py:28
  349.8 4.2 %collective-permute-done.19 = f32[1,34,1,128]{3,2,1,0:T(1,128)S(1)} collective-permute-done((f32[1,34,1,128]{3,2,1,0:T(1,128)S(1)}, f32[1,34,1,128]{3,2,1,0:T(1,128)S(1)}, u32[]{:S(2)}, u32[]{:S(2)}) %collective-permute-start.19) | collective-permute-done | bytes 17440 | tf_op jit(solution)/shard_map/ppermute | solution.py:28
  356.1 3.1 copy.53
  (118 shorter events, 75.1 us)
Async XLA Ops:
  7.2 63.9 %copy-start = (f32[32,32,4,128]{3,2,1,0:T(4,128)S(1)}, f32[32,32,4,128]{3,2,1,0:T(4,128)}, u32[]{:S(2)}) copy-start(f32[32,32,4,128]{3,2,1,0:T(4,128)} %param.2) | copy-start | bytes 6291460
  7.2 61.1 %all-reduce.13.cloned.1.call-start = ((), (), s32[]{:S(2)}) async-start(), calls=%async_computation | async-start | bytes 131072 | tf_op jit(solution)/shard_map/psum | solution.py:169
  9.9 174.1 %all-reduce.15.cloned.1.call-start = ((), (), s32[]{:S(2)}) async-start(), calls=%async_computation.1 | async-start | bytes 131072 | tf_op jit(solution)/shard_map/psum | solution.py:169
  74.3 7.3 %collective-permute-start = (f32[34,2,4,128]{3,1,2,0:T(2,128)S(1)}, f32[34,2,4,128]{3,1,2,0:T(2,128)S(1)}, u32[]{:S(2)}, u32[]{:S(2)}) collective-permute-start(f32[34,2,4,128]{3,1,2,0:T(2,128)S(1)} %get-tuple-element.44), channel_id=1, source_target_pairs={{0,2},{1,3},{4,6},{5,7},{8,10},{9,11},{12,14},{13,15},{16,18},{17,... | collective-permute-start | bytes 417800 | tf_op jit(solution)/shard_map/ppermute | solution.py:26
  77.6 6.9 %collective-permute-start.1 = (f32[34,2,4,128]{3,1,2,0:T(2,128)S(1)}, f32[34,2,4,128]{3,1,2,0:T(2,128)S(1)}, u32[]{:S(2)}, u32[]{:S(2)}) collective-permute-start(f32[34,2,4,128]{3,1,2,0:T(2,128)S(1)} %get-tuple-element.45), channel_id=1, source_target_pairs={{2,0},{3,1},{6,4},{7,5},{10,8},{11,9},{14,12},{15,13},{18,16},{19,... | collective-permute-start | bytes 417800 | tf_op jit(solution)/shard_map/ppermute | solution.py:28
  85.2 30.0 %collective-permute-start.2 = (f32[34,36,2,128]{3,1,2,0:T(8,128)S(1)}, f32[34,36,2,128]{3,1,2,0:T(8,128)S(1)}, u32[]{:S(2)}, u32[]{:S(2)}) collective-permute-start(f32[34,36,2,128]{3,1,2,0:T(8,128)S(1)} %get-tuple-element.33), channel_id=1, source_target_pairs={{0,1},{2,3},{4,5},{6,7},{8,9},{10,11},{12,13},{14,15},{16,17},{18,... | collective-permute-start | bytes 3760136 | tf_op jit(solution)/shard_map/ppermute | solution.py:26
  88.7 30.7 %collective-permute-start.3 = (f32[34,36,2,128]{3,1,2,0:T(8,128)S(1)}, f32[34,36,2,128]{3,1,2,0:T(8,128)S(1)}, u32[]{:S(2)}, u32[]{:S(2)}) collective-permute-start(f32[34,36,2,128]{3,1,2,0:T(8,128)S(1)} %get-tuple-element.32), channel_id=1, source_target_pairs={{1,0},{3,2},{5,4},{7,6},{9,8},{11,10},{13,12},{15,14},{17,16},{19,... | collective-permute-start | bytes 3760136 | tf_op jit(solution)/shard_map/ppermute | solution.py:28
  130.9 171.6 %all-reduce.17.cloned.1.call-start = ((), (), s32[]{:S(2)}) async-start(), calls=%async_computation.2 | async-start | bytes 524288 | tf_op jit(solution)/shard_map/psum | solution.py:178
  189.8 7.5 %collective-permute-start.4 = (f32[34,2,4,128]{3,1,2,0:T(2,128)S(1)}, f32[34,2,4,128]{3,1,2,0:T(2,128)S(1)}, u32[]{:S(2)}, u32[]{:S(2)}) collective-permute-start(f32[34,2,4,128]{3,1,2,0:T(2,128)S(1)} %get-tuple-element.40), channel_id=1, source_target_pairs={{0,2},{1,3},{4,6},{5,7},{8,10},{9,11},{12,14},{13,15},{16,18},{17,... | collective-permute-start | bytes 417800 | tf_op jit(solution)/shard_map/ppermute | solution.py:26
  193.2 6.9 %collective-permute-start.5 = (f32[34,2,4,128]{3,1,2,0:T(2,128)S(1)}, f32[34,2,4,128]{3,1,2,0:T(2,128)S(1)}, u32[]{:S(2)}, u32[]{:S(2)}) collective-permute-start(f32[34,2,4,128]{3,1,2,0:T(2,128)S(1)} %get-tuple-element.41), channel_id=1, source_target_pairs={{2,0},{3,1},{6,4},{7,5},{10,8},{11,9},{14,12},{15,13},{18,16},{19,... | collective-permute-start | bytes 417800 | tf_op jit(solution)/shard_map/ppermute | solution.py:28
  200.8 30.0 %collective-permute-start.6 = (f32[34,36,2,128]{3,1,2,0:T(8,128)S(1)}, f32[34,36,2,128]{3,1,2,0:T(8,128)S(1)}, u32[]{:S(2)}, u32[]{:S(2)}) collective-permute-start(f32[34,36,2,128]{3,1,2,0:T(8,128)S(1)} %get-tuple-element.31), channel_id=1, source_target_pairs={{0,1},{2,3},{4,5},{6,7},{8,9},{10,11},{12,13},{14,15},{16,17},{18,... | collective-permute-start | bytes 3760136 | tf_op jit(solution)/shard_map/ppermute | solution.py:26
  204.3 30.7 %collective-permute-start.7 = (f32[34,36,2,128]{3,1,2,0:T(8,128)S(1)}, f32[34,36,2,128]{3,1,2,0:T(8,128)S(1)}, u32[]{:S(2)}, u32[]{:S(2)}) collective-permute-start(f32[34,36,2,128]{3,1,2,0:T(8,128)S(1)} %get-tuple-element.30), channel_id=1, source_target_pairs={{1,0},{3,2},{5,4},{7,6},{9,8},{11,10},{13,12},{15,14},{17,16},{19,... | collective-permute-start | bytes 3760136 | tf_op jit(solution)/shard_map/ppermute | solution.py:28
  303.2 5.6 %collective-permute-start.8 = (f32[3,1,4,128]{3,2,1,0:T(4,128)S(1)}, f32[3,1,4,128]{3,2,1,0:T(4,128)S(1)}, u32[]{:S(2)}, u32[]{:S(2)}) collective-permute-start(f32[3,1,4,128]{3,2,1,0:T(4,128)S(1)} %get-tuple-element.49), channel_id=1, source_target_pairs={{0,2},{1,3},{4,6},{5,7},{8,10},{9,11},{12,14},{13,15},{16,18},{17,... | collective-permute-start | bytes 18440 | tf_op jit(solution)/shard_map/ppermute | solution.py:26
  306.6 5.5 %collective-permute-start.9 = (f32[3,1,4,128]{3,2,1,0:T(4,128)S(1)}, f32[3,1,4,128]{3,2,1,0:T(4,128)S(1)}, u32[]{:S(2)}, u32[]{:S(2)}) collective-permute-start(f32[3,1,4,128]{3,2,1,0:T(4,128)S(1)} %get-tuple-element.50), channel_id=1, source_target_pairs={{2,0},{3,1},{6,4},{7,5},{10,8},{11,9},{14,12},{15,13},{18,16},{19,... | collective-permute-start | bytes 18440 | tf_op jit(solution)/shard_map/ppermute | solution.py:28
  312.2 5.8 %collective-permute-start.10 = (f32[3,34,1,128]{3,2,1,0:T(1,128)S(1)}, f32[3,34,1,128]{3,2,1,0:T(1,128)S(1)}, u32[]{:S(2)}, u32[]{:S(2)}) collective-permute-start(f32[3,34,1,128]{3,2,1,0:T(1,128)S(1)} %get-tuple-element.51), channel_id=1, source_target_pairs={{0,1},{2,3},{4,5},{6,7},{8,9},{10,11},{12,13},{14,15},{16,17},{18,... | collective-permute-start | bytes 156680 | tf_op jit(solution)/shard_map/ppermute | solution.py:26
  315.6 6.0 %collective-permute-start.11 = (f32[3,34,1,128]{3,2,1,0:T(1,128)S(1)}, f32[3,34,1,128]{3,2,1,0:T(1,128)S(1)}, u32[]{:S(2)}, u32[]{:S(2)}) collective-permute-start(f32[3,34,1,128]{3,2,1,0:T(1,128)S(1)} %get-tuple-element.52), channel_id=1, source_target_pairs={{1,0},{3,2},{5,4},{7,6},{9,8},{11,10},{13,12},{15,14},{17,16},{19,... | collective-permute-start | bytes 156680 | tf_op jit(solution)/shard_map/ppermute | solution.py:28
  324.1 3.0 collective-permute-start.12
  325.8 5.5 %collective-permute-start.13 = (f32[1,1,4,128]{3,2,1,0:T(4,128)S(1)}, f32[1,1,4,128]{3,2,1,0:T(4,128)S(1)}, u32[]{:S(2)}, u32[]{:S(2)}) collective-permute-start(f32[1,1,4,128]{3,2,1,0:T(4,128)S(1)} %get-tuple-element.60), channel_id=1, source_target_pairs={{2,0},{3,1},{6,4},{7,5},{10,8},{11,9},{14,12},{15,13},{18,16},{19,... | collective-permute-start | bytes 6152 | tf_op jit(solution)/shard_map/ppermute | solution.py:28
  331.3 3.0 collective-permute-start.14
  332.9 5.6 %collective-permute-start.15 = (f32[1,34,1,128]{3,2,1,0:T(1,128)S(1)}, f32[1,34,1,128]{3,2,1,0:T(1,128)S(1)}, u32[]{:S(2)}, u32[]{:S(2)}) collective-permute-start(f32[1,34,1,128]{3,2,1,0:T(1,128)S(1)} %get-tuple-element.56), channel_id=1, source_target_pairs={{1,0},{3,2},{5,4},{7,6},{9,8},{11,10},{13,12},{15,14},{17,16},{19,... | collective-permute-start | bytes 52232 | tf_op jit(solution)/shard_map/ppermute | solution.py:28
  339.6 3.0 collective-permute-start.16
  341.2 5.5 %collective-permute-start.17 = (f32[1,1,4,128]{3,2,1,0:T(4,128)S(1)}, f32[1,1,4,128]{3,2,1,0:T(4,128)S(1)}, u32[]{:S(2)}, u32[]{:S(2)}) collective-permute-start(f32[1,1,4,128]{3,2,1,0:T(4,128)S(1)} %get-tuple-element.58), channel_id=1, source_target_pairs={{2,0},{3,1},{6,4},{7,5},{10,8},{11,9},{14,12},{15,13},{18,16},{19,... | collective-permute-start | bytes 6152 | tf_op jit(solution)/shard_map/ppermute | solution.py:28
  346.8 3.1 collective-permute-start.18
  348.4 5.6 %collective-permute-start.19 = (f32[1,34,1,128]{3,2,1,0:T(1,128)S(1)}, f32[1,34,1,128]{3,2,1,0:T(1,128)S(1)}, u32[]{:S(2)}, u32[]{:S(2)}) collective-permute-start(f32[1,34,1,128]{3,2,1,0:T(1,128)S(1)} %get-tuple-element.54), channel_id=1, source_target_pairs={{1,0},{3,2},{5,4},{7,6},{9,8},{11,10},{13,12},{15,14},{17,16},{19,... | collective-permute-start | bytes 52232 | tf_op jit(solution)/shard_map/ppermute | solution.py:28
  (3 other events, 36.4 us)
Sparse Core Ops, SparseCore 0:
  10.9 57.4 all-reduce.12
  131.0 52.9 all-reduce.14
  248.8 53.7 all-reduce.16
where the time goes:
time: 367 us; the launch traced here: 366 us
  waiting for transfers between devices  245 us (67%)
  other arithmetic  55.6 us (15%)
  starting transfers between devices  40.7 us (11%)
  between operations  14.5 us (4%)
  local copies, waits for them, and re-layouts  10.4 us (3%)
    psum x2, waiting for transfers between devices, local(): local_temp = lax.psum(jnp.sum(current, 0) / NORD, 'ord')  109 us
    psum x1, waiting for transfers between devices, local(): shares = lax.psum(partial_value, 'ord')  53.9 us
    ppermute x10, waiting for transfers between devices, extended(): lax.ppermute(tail, axis, [(i, (i + 1) % count) for i in range(ends)])  43.7 us
    ppermute x10, waiting for transfers between devices, extended(): lax.ppermute(head, axis, [((i + 1) % count, i) for i in range(ends)])  37.9 us
    ppermute x10, starting transfers between devices, extended(): lax.ppermute(tail, axis, [(i, (i + 1) % count) for i in range(ends)])  27 us
    div x6, other arithmetic, axis_flux(): (lower_diff * (upper_diff * upper_diff + limiter_eps) + upper_diff * (low...  14.3 us
    ppermute x10, starting transfers between devices, extended(): lax.ppermute(head, axis, [((i + 1) % count, i) for i in range(ends)])  13.6 us
    div x6, other arithmetic, axis_flux(): (2.0 * relax_face * upwind + 0.5 * time_step * temp_face) / (2.0 * relax_...  11.4 us
  transfers between devices with their start and end apart: 23, of which 17 were waited for; matrix products, arithmetic and copies ran while one was open for 4% of the time, Pallas kernels for 0%

commit v1 on v0

v1 whole, which is shorter than its diff:
```python
import jax
import jax.numpy as jnp
from jax import lax
from jax.experimental import pallas as pl
from jax.experimental.pallas import tpu as pltpu
from jax.sharding import PartitionSpec as P

NORD = 256
STEPS = 2
SWEEPS = 3
LANE_GROUP = 8

h = 0.4
eps = 0.01
diffusion_mass = 0.5
flux_weight = 2.0
golden_turn = 2.399963229728653
MESH = pl.DeviceIdType.MESH
f32 = jnp.float32


def directions(offset, length):
    ordinal = (offset + jnp.arange(length, dtype=jnp.int32)).astype(jnp.float32)
    height = 1.0 - (2.0 * ordinal + 1.0) / NORD
    radius = jnp.sqrt(1.0 - height * height)
    turned = golden_turn * ordinal
    return jnp.stack([radius * jnp.cos(turned), radius * jnp.sin(turned), height])


def slope_of(a, b, aa, bb):
    return (a + b) * (a * b + eps) / (aa + bb)


def kernel(dims, speed, dist, relax, out, temp_out, *scratch):
    NO, NX, NY, O, X, Y, Z = dims
    (q0, q1, q2, src, hx, hy, acc, tmix, te, re, pe, fxe, fye, drv, px, qx, py, qy, pzh, pzl, dqz,
     ca, cb, part, rbuf, full, ssx, ssy, hsx, hsy, b_send, b_recv, s_send, s_recv, p_send, p_recv) = scratch
    G = O // LANE_GROUP
    N = X * Y
    R = N // NO
    U = LANE_GROUP
    XO = 8
    mo, mx, my = lax.axis_index("ord"), lax.axis_index("gx"), lax.axis_index("gy")
    has = (mx > 0, mx < NX - 1, my > 0, my < NY - 1)
    peer = ({"gx": mx - 1}, {"gx": mx + 1}, {"gy": my - 1}, {"gy": my + 1})

    barrier = pltpu.get_barrier_semaphore()
    for k in range(1, NO):
        pl.semaphore_signal(barrier, inc=1, device_id={"ord": lax.rem(mo + k, NO)}, device_id_type=MESH)
    for side in range(4):
        @pl.when(has[side])
        def _():
            pl.semaphore_signal(barrier, inc=1, device_id=peer[side], device_id_type=MESH)
    ends = sum((jnp.where(flag, 1, 0) for flag in has), 0)
    pl.semaphore_wait(barrier, NO - 1 + ends)

    def small_copy(ev, layers, side):
        buf_s, buf_r = (ssx, hsx) if side < 2 else (ssy, hsy)
        mine, theirs = side % 2, 1 - side % 2
        return pltpu.make_async_remote_copy(
            src_ref=buf_s.at[ev, mine, pl.ds(0, layers)],
            dst_ref=buf_r.at[ev, theirs, pl.ds(0, layers)],
            send_sem=s_send.at[ev, side],
            recv_sem=s_recv.at[ev, side ^ 1],
            device_id=peer[side], device_id_type=MESH)

    def small_recv(ev, layers, side):
        buf_s, buf_r = (ssx, hsx) if side < 2 else (ssy, hsy)
        return pltpu.make_async_remote_copy(
            src_ref=buf_s.at[ev, side % 2, pl.ds(0, layers)],
            dst_ref=buf_r.at[ev, side % 2, pl.ds(0, layers)],
            send_sem=s_send.at[ev, side],
            recv_sem=s_recv.at[ev, side],
            device_id=peer[side], device_id_type=MESH)

    def small_start(ev, layers, fx, fy):
        for l in range(layers):
            for y in range(Y):
                ssx[ev, 0, l, y:y + 1, :] = fx[y + 2, XO + l:XO + l + 1, :]
                ssx[ev, 1, l, y:y + 1, :] = fx[y + 2, XO + X - layers + l:XO + X - layers + l + 1, :]
            ssy[ev, 0, l] = fy[2 + l, XO:XO + X, :]
            ssy[ev, 1, l] = fy[2 + Y - layers + l, XO:XO + X, :]
        for side in range(4):
            @pl.when(has[side])
            def _():
                small_copy(ev, layers, side).start()

    def small_finish(ev, layers, fx, fy):
        for side in range(4):
            @pl.when(has[side])
            def _():
                small_recv(ev, layers, side).wait_recv()
                for l in range(layers):
                    if side < 2:
                        at = XO - layers + l if side == 0 else XO + X + l
                        for y in range(Y):
                            fx[y + 2, at:at + 1, :] = hsx[ev, side % 2, l, y:y + 1, :]
                    else:
                        at = 2 - layers + l if side == 2 else 2 + Y + l
                        fy[at, XO:XO + X, :] = hsy[ev, side % 2, l]

    bigs = (q0, q1)

    def big(t, g, side, sending):
        q = bigs[t]
        if side < 2:
            lo = 0 if side == 0 else X - 2
            s = q.at[g, :, pl.ds(lo, 2)]
            buf = hx
        else:
            lo = 0 if side == 2 else Y - 2
            s = q.at[g, pl.ds(lo, 2)]
            buf = hy
        slot = (1 - side % 2) if sending else side % 2
        return pltpu.make_async_remote_copy(
            src_ref=s, dst_ref=buf.at[t, slot, g],
            send_sem=b_send.at[t, g, side],
            recv_sem=b_recv.at[t, g, side ^ 1 if sending else side],
            device_id=peer[side], device_id_type=MESH)

    def psum_scatter_copy(ev, fields, k):
        to = lax.rem(mo + k, NO)
        return pltpu.make_async_remote_copy(
            src_ref=part.at[ev, to, pl.ds(0, fields)], dst_ref=rbuf.at[ev, k, pl.ds(0, fields)],
            send_sem=p_send.at[ev, 0, k], recv_sem=p_recv.at[ev, 0, k],
            device_id={"ord": to}, device_id_type=MESH)

    def psum_gather_copy(ev, fields, k, owner):
        to = lax.rem(mo + k, NO)
        return pltpu.make_async_remote_copy(
            src_ref=full.at[ev, mo, pl.ds(0, fields)], dst_ref=full.at[ev, owner, pl.ds(0, fields)],
            send_sem=p_send.at[ev, 1, k], recv_sem=p_recv.at[ev, 1, k],
            device_id={"ord": to}, device_id_type=MESH)

    def psum_start(ev, fields):
        for k in range(1, NO):
            psum_scatter_copy(ev, fields, k).start()

    def psum_finish(ev, fields):
        for k in range(1, NO):
            psum_scatter_copy(ev, fields, k).wait_recv()
        for f in range(fields):
            total = part[ev, mo, f]
            for k in range(1, NO):
                total = total + rbuf[ev, k, f]
            full[ev, mo, f] = total * (1.0 / NORD)
        for k in range(1, NO):
            psum_gather_copy(ev, fields, k, mo).start()
        for k in range(1, NO):
            psum_gather_copy(ev, fields, k, lax.rem(mo + NO - k, NO)).wait_recv()

    def rows(r):
        return r // R, r % R

    def unpack(ev, f, dst):
        for y in range(Y):
            for n in range(max(1, X // R)):
                size = min(R, X)
                r0 = y * X + n * size
                dst[y + 2, XO + n * size:XO + (n + 1) * size, :] = full[ev, r0 // R, f, r0 % R:r0 % R + size, :]

    def put_plane(ev, f, y, value):
        size = min(R, X)
        for n in range(X // size):
            r0 = y * X + n * size
            part[ev, r0 // R, f, r0 % R:r0 % R + size, :] = value[n * size:(n + 1) * size]

    for ref in (te, re, pe, fxe, fye):
        ref[...] = jnp.zeros_like(ref)
    for y in range(Y):
        re[y + 2, XO:XO + X, :] = relax[pl.ds(y, X, stride=Y), :]
    small_start(0, 2, re, re)

    @pl.loop(0, G)
    def _(g):
        @pl.loop(0, X)
        def _(x):
            for y in range(Y):
                q0[g, y, x] = dist[pl.ds(g * U * N + x * Y + y, U, stride=N), :]
        for side in range(4):
            @pl.when(has[side])
            def _():
                big(0, g, side, True).start()

    @pl.loop(0, N // 8)
    def _(i):
        at = pl.multiple_of(i * 8, 8)
        total = dist[pl.ds(at, 8), :]
        for o in range(1, O):
            total = total + dist[pl.ds(o * N + at, 8), :]
        tmix[pl.ds(at, 8), :] = total
    for y in range(Y):
        put_plane(0, 0, y, tmix[pl.ds(y, X, stride=Y), :])
    psum_start(0, 1)

    src[...] = jnp.zeros_like(src)
    small_finish(0, 2, re, re)
    lane = lax.broadcasted_iota(jnp.int32, (X, Z), 1)

    def shift_up(v):
        return jnp.where(lane == Z - 1, 0.0, pltpu.roll(v, Z - 1, 1))

    def shift_down(v):
        return jnp.where(lane == 0, 0.0, pltpu.roll(v, 1, 1))

    XA = X + 2 * XO

    def face_r(r0, r1):
        r = 0.5 * (r0 + r1)
        return 2.0 * r / (2.0 * r + 0.5 * h)

    def face_t(t0, t1, p):
        return 0.5 * (t0 + t1) * (1.0 - p)

    for y in range(Y + 4):
        r = re[y]
        ca[y] = (2.0 * r - h) / (2.0 * r + h)
    for y in range(Y):
        r = re[y + 2, XO:XO + X, :]
        px[y, 0:X, :] = face_r(re[y + 2, XO - 1:XO - 1 + X, :], r)
        px[y, X:X + 1, :] = face_r(re[y + 2, XO + X - 1:XO + X, :], re[y + 2, XO + X:XO + X + 1, :])
        pzh[y] = face_r(r, shift_up(r))
        pzl[y] = face_r(shift_down(r), r)
    for y in range(Y + 1):
        py[y] = face_r(re[y + 1, XO:XO + X, :], re[y + 2, XO:XO + X, :])

    def coefficients():
        for y in range(Y + 4):
            cb[y] = 2.0 * h * te[y] / (2.0 * re[y] + h)
        for y in range(Y):
            t = te[y + 2, XO:XO + X, :]
            qx[y, 0:X, :] = face_t(te[y + 2, XO - 1:XO - 1 + X, :], t, px[y, 0:X, :])
            qx[y, X:X + 1, :] = face_t(te[y + 2, XO + X - 1:XO + X, :], te[y + 2, XO + X:XO + X + 1, :], px[y, X:X + 1, :])
            dqz[y] = face_t(t, shift_up(t), pzh[y]) - face_t(shift_down(t), t, pzl[y])
        for y in range(Y + 1):
            qy[y] = face_t(te[y + 1, XO:XO + X, :], te[y + 2, XO:XO + X, :], py[y])

    def row(ref, y, x):
        return jnp.broadcast_to(ref[y, pl.ds(x, 1), :], (U, Z))

    lane8 = lax.broadcasted_iota(jnp.int32, (U, Z), 1)

    def advance(t, g):
        q, qn = (q0, q1, q2)[t], (q0, q1, q2)[t + 1]

        @pl.loop(0, X)
        def _(x):
            for y in range(Y):
                src[y + 2, x + 2] = row(ca, y + 2, XO + x) * q[g, y, x] + row(cb, y + 2, XO + x)
        for side in range(4):
            @pl.when(has[side])
            def _():
                big(t, g, side, False).wait_recv()
                if side < 2:
                    for l in range(2):
                        x = (l - 2) if side == 0 else X + l
                        for y in range(Y):
                            src[y + 2, x + 2] = row(ca, y + 2, XO + x) * hx[t, side, g, y, l] + row(cb, y + 2, XO + x)
                else:
                    @pl.loop(0, X)
                    def _(x):
                        for l in range(2):
                            y = (l - 2) if side == 2 else Y + l
                            src[y + 2, x + 2] = row(ca, y + 2, XO + x) * hy[t, side - 2, g, l, x] + row(cb, y + 2, XO + x)

        cx, cy, cz = speed[0, g], speed[1, g], speed[2, g]

        def gamma(c):
            return jnp.where(c >= 0.0, 0.5 * (1.0 - h * c), -0.5 * (1.0 + h * c))

        gx_, gy_, gz_ = gamma(cx), gamma(cy), gamma(cz)
        gz_abs = jnp.abs(gz_)
        hcx, hcy, hcz = h * cx, h * cy, h * cz

        start = []
        for y in range(Y):
            sm2, sm1, s0, s1 = (src[y + 2, i] for i in range(4))
            a, b, c = sm1 - sm2, s0 - sm1, s1 - s0
            aa, bb, cc = a * a + eps, b * b + eps, c * c + eps
            um = sm1 + gx_ * slope_of(a, b, aa, bb)
            u0 = s0 + gx_ * slope_of(b, c, bb, cc)
            e0 = row(px, y, 0) * jnp.where(cx >= 0.0, um, u0) + row(qx, y, 0)
            start += [u0, e0, c]

        def body(x, carry):
            posx, posy, posz = cx >= 0.0, cy >= 0.0, cz >= 0.0
            column = [src[j, x + 2] for j in range(Y + 4)]
            d = [column[j + 1] - column[j] for j in range(Y + 3)]
            e = [v * v + eps for v in d]
            u = [None] + [column[j] + gy_ * slope_of(d[j - 1], d[j], e[j - 1], e[j]) for j in range(1, Y + 3)]
            ey = [row(py, f, x) * jnp.where(posy, u[f + 1], u[f + 2]) + row(qy, f, x) for f in range(Y + 1)]
            carried = []
            for y in range(Y):
                s = column[y + 2]
                u0, e0, c = carry[3 * y:3 * y + 3]
                s1, s2 = src[y + 2, x + 3], src[y + 2, x + 4]
                d1 = s2 - s1
                u1 = s1 + gx_ * slope_of(c, d1, c * c + eps, d1 * d1 + eps)
                e1 = row(px, y, x + 1) * jnp.where(posx, u0, u1) + row(qx, y, x + 1)
                carried += [u1, e1, d1]
                za = s - jnp.where(lane8 == 0, 0.0, pltpu.roll(s, 1, 1))
                zb = jnp.where(lane8 == Z - 1, 0.0, pltpu.roll(s, Z - 1, 1)) - s
                uz = s + gz_ * slope_of(za, zb, za * za + eps, zb * zb + eps)
                ghost = gz_abs * (s * eps / (s * s + 2.0 * eps))
                wl = jnp.where(lane8 == 0, ghost, pltpu.roll(uz, 1, 1))
                wr = jnp.where(lane8 == Z - 1, ghost, pltpu.roll(uz, Z - 1, 1))
                up_hi = jnp.where(posz, uz, wr)
                up_lo = jnp.where(posz, wl, uz)
                fz = row(pzh, y, x) * up_hi - row(pzl, y, x) * up_lo + row(dqz, y, x)
                new = s - (hcx * (e1 - e0) + hcy * (ey[y + 1] - ey[y]) + hcz * fz)
                qn[g, y, x] = new
                if t == 0:
                    acc[0, y, x] += new
                else:
                    acc[0, y, x] += new
                    acc[1, y, x] += cx * new
                    acc[2, y, x] += cy * new
                    acc[3, y, x] += cz * new
            return tuple(carried)

        lax.fori_loop(0, X, body, tuple(start))

    def fold(f, y, dst):
        @pl.loop(0, X)
        def _(x):
            dst[y, pl.ds(XO + x, 1), :] = jnp.sum(acc[f, y, x], axis=0, keepdims=True)

    for t in range(STEPS):
        psum_finish(t, 1)
        unpack(t, 0, te)
        small_start(1 + t, 2, te, te)
        acc[...] = jnp.zeros_like(acc)
        small_finish(1 + t, 2, te, te)
        coefficients()

        @pl.loop(0, G)
        def _(g):
            advance(t, g)
            if t + 1 < STEPS:
                for side in range(4):
                    @pl.when(has[side])
                    def _():
                        big(t + 1, g, side, True).start()

        if t + 1 < STEPS:
            for y in range(Y):
                fold(0, y, drv)
                put_plane(t + 1, 0, y, drv[y, XO:XO + X, :])
            psum_start(t + 1, 1)

    for y in range(Y):
        for f, dst, at in ((1, fxe, y + 2), (2, fye, y + 2), (0, te, y), (3, drv, y)):
            @pl.loop(0, X)
            def _(x):
                dst[at, pl.ds(XO + x, 1), :] = jnp.sum(acc[f, y, x], axis=0, keepdims=True)
    small_start(3, 1, fxe, fye)
    small_finish(3, 1, fxe, fye)
    for y in range(Y):
        fz = drv[y, XO:XO + X, :]
        energy = te[y, XO:XO + X, :]
        spread = 0.5 * (fxe[y + 2, XO + 1:XO + 1 + X, :] - fxe[y + 2, XO - 1:XO - 1 + X, :])
        spread = spread + 0.5 * (fye[y + 3, XO:XO + X, :] - fye[y + 1, XO:XO + X, :])
        spread = spread + 0.5 * (shift_up(fz) - shift_down(fz))
        put_plane(2, 0, y, energy)
        put_plane(2, 1, y, energy - flux_weight * spread)
    psum_start(2, 2)
    psum_finish(2, 2)
    unpack(2, 0, pe)
    unpack(2, 1, fye)
    for sweep in range(SWEEPS):
        small_start(4 + sweep, 1, pe, pe)
        small_finish(4 + sweep, 1, pe, pe)
        potential = []
        for y in range(Y):
            p = pe[y + 2, XO:XO + X, :]
            k = 1.0 / (1.0 + p * p)
            weighted = diffusion_mass * fye[y + 2, XO:XO + X, :]
            weights = jnp.full_like(p, diffusion_mass)
            for n in (pe[y + 2, XO - 1:XO - 1 + X, :], pe[y + 2, XO + 1:XO + 1 + X, :],
                      pe[y + 1, XO:XO + X, :], pe[y + 3, XO:XO + X, :], shift_down(p), shift_up(p)):
                couple = 0.5 * (k + 1.0 / (1.0 + n * n))
                weighted = weighted + couple * n
                weights = weights + couple
            potential.append(weighted / weights)
        for y in range(Y):
            pe[y + 2, XO:XO + X, :] = potential[y]

    for y in range(Y):
        value = pe[y + 2, XO:XO + X, :]
        temp_out[pl.ds(y, X, stride=Y), :] = value
        cb[y + 2, XO:XO + X, :] = 2.0 * h * value / (2.0 * re[y + 2, XO:XO + X, :] + h)

    @pl.loop(0, X)
    def _(x):
        for y in range(Y):
            a, b = row(ca, y + 2, XO + x), row(cb, y + 2, XO + x)
            for g in range(G):
                out[pl.ds(g * U * N + x * Y + y, U, stride=N), :] = a * q2[g, y, x] + b

    for side in range(4):
        @pl.when(has[side])
        def _():
            for ev in range(4 + SWEEPS):
                small_copy(ev, 2 if ev < 3 else 1, side).wait_send()
            for t in range(2):
                @pl.loop(0, G)
                def _(g):
                    big(t, g, side, True).wait_send()
    for ev in range(3):
        for k in range(1, NO):
            psum_scatter_copy(ev, 2 if ev == 2 else 1, k).wait_send()
            psum_gather_copy(ev, 2 if ev == 2 else 1, k, mo).wait_send()


def solution(mesh):
    NO, NX, NY = (mesh.shape[name] for name in ("ord", "gx", "gy"))

    def local(distribution, relaxation):
        O, X, Y, Z = distribution.shape
        G, U, N = O // LANE_GROUP, LANE_GROUP, X * Y
        R = N // NO
        speeds = directions(lax.axis_index("ord") * O, O)
        speeds = jnp.broadcast_to(speeds.reshape(3, G, U, 1), (3, G, U, Z))
        XA = X + 16
        v = lambda *s: pltpu.VMEM(s, f32)
        dma = lambda *s: pltpu.SemaphoreType.DMA(s)
        import functools
        scratch = [
            v(G, Y, X, U, Z), v(G, Y, X, U, Z), v(G, Y, X, U, Z), v(Y + 4, X + 4, U, Z),
            v(2, 2, G, Y, 2, U, Z), v(2, 2, G, 2, X, U, Z), v(4, Y, X, U, Z), v(N, Z),
            v(Y + 4, XA, Z), v(Y + 4, XA, Z), v(Y + 4, XA, Z), v(Y + 4, XA, Z), v(Y + 4, XA, Z), v(Y + 4, XA, Z),
            v(Y, X + 8, Z), v(Y, X + 8, Z), v(Y + 1, X, Z), v(Y + 1, X, Z), v(Y, X, Z), v(Y, X, Z), v(Y, X, Z),
            v(Y + 4, XA, Z), v(Y + 4, XA, Z),
            v(3, NO, 2, R, Z), v(3, NO, 2, R, Z), v(3, NO, 2, R, Z),
            v(4 + SWEEPS, 2, 2, Y, Z), v(4 + SWEEPS, 2, 2, X, Z), v(4 + SWEEPS, 2, 2, Y, Z), v(4 + SWEEPS, 2, 2, X, Z),
            dma(2, G, 4), dma(2, G, 4), dma(4 + SWEEPS, 4), dma(4 + SWEEPS, 4), dma(3, 2, NO), dma(3, 2, NO),
        ]
        updated, temperature = pl.pallas_call(
            functools.partial(kernel, (NO, NX, NY, O, X, Y, Z)),
            out_shape=(jax.ShapeDtypeStruct((O * N, Z), f32), jax.ShapeDtypeStruct((N, Z), f32)),
            in_specs=[pl.BlockSpec(memory_space=pltpu.VMEM)] * 3,
            out_specs=[pl.BlockSpec(memory_space=pltpu.VMEM)] * 2,
            scratch_shapes=scratch,
            compiler_params=pltpu.CompilerParams(collective_id=0, has_side_effects=True, vmem_limit_bytes=48 * 2**20),
        )(speeds, distribution.reshape(O * N, Z), relaxation.reshape(N, Z))
        return updated.reshape(O, X, Y, Z), temperature.reshape(X, Y, Z)

    return jax.shard_map(
        local,
        mesh=mesh,
        in_specs=(P("ord", "gx", "gy", None), P("gx", "gy", None)),
        out_specs=(P("ord", "gx", "gy", None), P("gx", "gy", None)),
        check_vma=False,
    )
```

time: 367 us -> 125 us (0.34)
  waiting for transfers between devices: 245 us -> 0 us
  Pallas kernels: 0 us -> 119 us
  other arithmetic: 55.6 us -> 0.07 us
  starting transfers between devices: 40.7 us -> 0 us
  between operations: 14.5 us -> 0.65 us
  local copies, waits for them, and re-layouts: 10.4 us -> 4.46 us
    psum x3 -> x0, waiting for transfers between devices: 163 us -> none  [the longest x2 109 us: local(): local_temp = lax.psum(jnp.sum(current, 0) / NORD, 'ord')]
    pallas_call x0 -> x1, Pallas kernels: none -> 119 us  [local(): pl.pallas_call(functools.partial(kernel, (NO, NX, NY, O, X, Y, Z)), out_s...]
    ppermute x20 -> x0, waiting for transfers between devices: 81.6 us -> none  [the longest x10 43.7 us: extended(): lax.ppermute(tail, axis, [(i, (i + 1) % count) for i in range(ends)])]
    ppermute x20 -> x0, starting transfers between devices: 40.5 us -> none  [the longest x10 27 us: extended(): lax.ppermute(tail, axis, [(i, (i + 1) % count) for i in range(ends)])]
    div x21 -> x0, other arithmetic: 29.5 us -> none  [the longest x6 14.3 us: axis_flux(): (lower_diff * (upper_diff * upper_diff + limiter_eps) + upper_diff * (low...]
    concatenate x9 -> x0, other arithmetic: 10.7 us -> none  [the longest x7 10.2 us: extended(): jnp.concatenate([lax.ppermute(tail, axis, [(i, (i + 1) % count) for i in...]
    reduce_sum x4 -> x0, other arithmetic: 6.27 us -> none  [the longest x2 3.87 us: local(): local_temp = lax.psum(jnp.sum(current, 0) / NORD, 'ord')]
  transfers between devices with their start and end apart: 23 -> 0, of which waited for: 17 -> 0; matrix products, arithmetic and copies ran while one was open for 4% -> 0% of each run, Pallas kernels for 0% -> 0%
where the time goes in v1:
time: 125 us; the launch traced here: 124 us
  Pallas kernels  119 us (95%)
  local copies, waits for them, and re-layouts  4.46 us (4%)
    pallas_call x1, Pallas kernels, local(): pl.pallas_call(functools.partial(kernel, (NO, NX, NY, O, X, Y, Z)), out_s...  119 us
    unnamed x6, local copies, waits for them, and re-layouts  4.39 us

profile of v1, /device:TPU:0, one launch (start us, length us, event | category | flops | bytes accessed | tf_op | source)
XLA Modules:
  0.0 124.4 jit_solution(6490450345772563154)
XLA Ops:
  0.7 0.1 broadcast_in_dim.8.speed
  0.8 0.0 copy-start
  0.8 1.6 %copy-done = f32[32,32,4,128]{3,2,1,0:T(4,128)S(1)} copy-done((f32[32,32,4,128]{3,2,1,0:T(4,128)S(1)}, f32[32,32,4,128]{3,2,1,0:T(4,128)}, u32[]{:S(2)}) %copy-start) | copy-done | bytes 2097176
  2.4 0.0 copy-start.1
  2.4 0.8 copy-done.1
  3.2 119.2 %shard_map.41 = (f32[4096,128]{1,0:T(8,128)S(1)}, f32[128,128]{1,0:T(8,128)S(1)}) custom-call(f32[3,4,8,128]{3,2,1,0:T(8,128)S(1)} %broadcast_in_dim.8.speed, f32[4096,128]{1,0:T(8,128)S(1)} %bitcast.6, f32[128,128]{1,0:T(8,128)S(1)} %bitcast.8), custom_call_target="tpu_custom_call" | custom-call | tf_op jit(solution)/shard_map/pallas_call | solution.py:438
  122.4 1.3 %copy.6 = f32[32,32,4,128]{3,2,1,0:T(4,128)} copy(f32[32,32,4,128]{3,2,1,0:T(4,128)S(1)} %bitcast.7) | data formatting | bytes 4194304
  123.8 0.6 copy.7
  (3 shorter events, 0.1 us)
Async XLA Ops:
  0.8 1.6 %copy-start = (f32[32,32,4,128]{3,2,1,0:T(4,128)S(1)}, f32[32,32,4,128]{3,2,1,0:T(4,128)}, u32[]{:S(2)}) copy-start(f32[32,32,4,128]{3,2,1,0:T(4,128)} %param.2) | copy-start | bytes 6291460
  2.4 0.8 copy-start.1

commit v2 on v1

--- a/solution.py
+++ b/solution.py
@@ -33,7 +33,7 @@
 
 def kernel(dims, speed, dist, relax, out, temp_out, *scratch):
     NO, NX, NY, O, X, Y, Z = dims
-    (q0, q1, q2, src, hx, hy, acc, tmix, te, re, pe, fxe, fye, drv, px, qx, py, qy, pzh, pzl, dqz,
+    (q0, q1, q2, src, hx, hy, acc, tmix, te, re, pe, fxe, fye, drv, px, qx, py, qy, pz, dqz,
      ca, cb, part, rbuf, full, ssx, ssy, hsx, hsy, b_send, b_recv, s_send, s_recv, p_send, p_recv) = scratch
     G = O // LANE_GROUP
     N = X * Y
@@ -171,27 +171,42 @@
         re[y + 2, XO:XO + X, :] = relax[pl.ds(y, X, stride=Y), :]
     small_start(0, 2, re, re)
 
-    @pl.loop(0, G)
-    def _(g):
-        @pl.loop(0, X)
-        def _(x):
-            for y in range(Y):
-                q0[g, y, x] = dist[pl.ds(g * U * N + x * Y + y, U, stride=N), :]
-        for side in range(4):
-            @pl.when(has[side])
-            def _():
-                big(0, g, side, True).start()
-
     @pl.loop(0, N // 8)
     def _(i):
         at = pl.multiple_of(i * 8, 8)
-        total = dist[pl.ds(at, 8), :]
+        total = dist[0, pl.ds(at, 8), :]
         for o in range(1, O):
-            total = total + dist[pl.ds(o * N + at, 8), :]
+            total = total + dist[o, pl.ds(at, 8), :]
         tmix[pl.ds(at, 8), :] = total
     for y in range(Y):
         put_plane(0, 0, y, tmix[pl.ds(y, X, stride=Y), :])
     psum_start(0, 1)
+
+    def place(i, j):
+        if U % Y == 0:
+            return j % Y, i * (U // Y) + j // Y
+        return lax.rem(i * U + j, Y), (i * U + j) // Y
+
+    def big_start(t, g):
+        for side in range(4):
+            @pl.when(has[side])
+            def _():
+                big(t, g, side, True).start()
+
+    def transpose_in(g):
+        @pl.loop(0, N // U)
+        def _(i):
+            block = jnp.swapaxes(dist[pl.ds(g * U, U), pl.ds(pl.multiple_of(i * U, U), U), :], 0, 1)
+            for j in range(U):
+                y, x = place(i, j)
+                q0[g, y, x] = block[j]
+
+    transpose_in(0)
+    big_start(0, 0)
+
+    @pl.loop(1, G)
+    def _(g):
+        transpose_in(g)
 
     src[...] = jnp.zeros_like(src)
     small_finish(0, 2, re, re)
@@ -219,8 +234,8 @@
         r = re[y + 2, XO:XO + X, :]
         px[y, 0:X, :] = face_r(re[y + 2, XO - 1:XO - 1 + X, :], r)
         px[y, X:X + 1, :] = face_r(re[y + 2, XO + X - 1:XO + X, :], re[y + 2, XO + X:XO + X + 1, :])
-        pzh[y] = face_r(r, shift_up(r))
-        pzl[y] = face_r(shift_down(r), r)
+        pz[0, y] = face_r(r, shift_up(r))
+        pz[1, y] = face_r(shift_down(r), r)
     for y in range(Y + 1):
         py[y] = face_r(re[y + 1, XO:XO + X, :], re[y + 2, XO:XO + X, :])
 
@@ -231,7 +246,9 @@
             t = te[y + 2, XO:XO + X, :]
             qx[y, 0:X, :] = face_t(te[y + 2, XO - 1:XO - 1 + X, :], t, px[y, 0:X, :])
             qx[y, X:X + 1, :] = face_t(te[y + 2, XO + X - 1:XO + X, :], te[y + 2, XO + X:XO + X + 1, :], px[y, X:X + 1, :])
-            dqz[y] = face_t(t, shift_up(t), pzh[y]) - face_t(shift_down(t), t, pzl[y])
+            inflow = face_t(t, shift_up(t), pz[0, y]) - face_t(shift_down(t), t, pz[1, y])
+            dqz[0, y] = inflow
+            dqz[1, y] = -inflow
         for y in range(Y + 1):
             qy[y] = face_t(te[y + 1, XO:XO + X, :], te[y + 2, XO:XO + X, :], py[y])
 
@@ -243,7 +260,7 @@
     def advance(t, g):
         q, qn = (q0, q1, q2)[t], (q0, q1, q2)[t + 1]
 
-        @pl.loop(0, X)
+        @pl.loop(0, X, unroll=2)
         def _(x):
             for y in range(Y):
                 src[y + 2, x + 2] = row(ca, y + 2, XO + x) * q[g, y, x] + row(cb, y + 2, XO + x)
@@ -257,7 +274,7 @@
                         for y in range(Y):
                             src[y + 2, x + 2] = row(ca, y + 2, XO + x) * hx[t, side, g, y, l] + row(cb, y + 2, XO + x)
                 else:
-                    @pl.loop(0, X)
+                    @pl.loop(0, X, unroll=4)
                     def _(x):
                         for l in range(2):
                             y = (l - 2) if side == 2 else Y + l
@@ -269,8 +286,12 @@
             return jnp.where(c >= 0.0, 0.5 * (1.0 - h * c), -0.5 * (1.0 + h * c))
 
         gx_, gy_, gz_ = gamma(cx), gamma(cy), gamma(cz)
-        gz_abs = jnp.abs(gz_)
-        hcx, hcy, hcz = h * cx, h * cy, h * cz
+        gz_eps = jnp.abs(gz_) * eps
+        hcx, hcy, hcz = h * cx, h * cy, h * jnp.abs(cz)
+        upward = mo * O + g * U < NORD // 2
+        shift = jnp.where(upward, 1, Z - 1)
+        own = jnp.where(upward, 0, 1)
+        inlet = lane8 == jnp.where(upward, 0, Z - 1)
 
         start = []
         for y in range(Y):
@@ -283,11 +304,14 @@
             start += [u0, e0, c]
 
         def body(x, carry):
-            posx, posy, posz = cx >= 0.0, cy >= 0.0, cz >= 0.0
+            posx, posy = cx >= 0.0, cy >= 0.0
             column = [src[j, x + 2] for j in range(Y + 4)]
             d = [column[j + 1] - column[j] for j in range(Y + 3)]
-            e = [v * v + eps for v in d]
-            u = [None] + [column[j] + gy_ * slope_of(d[j - 1], d[j], e[j - 1], e[j]) for j in range(1, Y + 3)]
+            e = [None] + [d[j] * d[j] + eps for j in range(1, Y + 2)]
+            u = [None, None] + [column[j] + gy_ * slope_of(d[j - 1], d[j], e[j - 1], e[j]) for j in range(2, Y + 2)] + [None]
+            oa, ob = jnp.where(posy, d[0], d[Y + 1]), jnp.where(posy, d[1], d[Y + 2])
+            beyond = jnp.where(posy, column[1], column[Y + 2]) + gy_ * slope_of(oa, ob, oa * oa + eps, ob * ob + eps)
+            u[1] = u[Y + 2] = beyond
             ey = [row(py, f, x) * jnp.where(posy, u[f + 1], u[f + 2]) + row(qy, f, x) for f in range(Y + 1)]
             carried = []
             for y in range(Y):
@@ -298,15 +322,12 @@
                 u1 = s1 + gx_ * slope_of(c, d1, c * c + eps, d1 * d1 + eps)
                 e1 = row(px, y, x + 1) * jnp.where(posx, u0, u1) + row(qx, y, x + 1)
                 carried += [u1, e1, d1]
-                za = s - jnp.where(lane8 == 0, 0.0, pltpu.roll(s, 1, 1))
                 zb = jnp.where(lane8 == Z - 1, 0.0, pltpu.roll(s, Z - 1, 1)) - s
+                za = jnp.where(lane8 == 0, s, pltpu.roll(zb, 1, 1))
                 uz = s + gz_ * slope_of(za, zb, za * za + eps, zb * zb + eps)
-                ghost = gz_abs * (s * eps / (s * s + 2.0 * eps))
-                wl = jnp.where(lane8 == 0, ghost, pltpu.roll(uz, 1, 1))
-                wr = jnp.where(lane8 == Z - 1, ghost, pltpu.roll(uz, Z - 1, 1))
-                up_hi = jnp.where(posz, uz, wr)
-                up_lo = jnp.where(posz, wl, uz)
-                fz = row(pzh, y, x) * up_hi - row(pzl, y, x) * up_lo + row(dqz, y, x)
+                ghost = gz_eps * s / (s * s + 2.0 * eps)
+                wz = jnp.where(inlet, ghost, pltpu.roll(uz, shift, 1))
+                fz = row(pz.at[own], y, x) * uz - row(pz.at[1 - own], y, x) * wz + row(dqz.at[own], y, x)
                 new = s - (hcx * (e1 - e0) + hcy * (ey[y + 1] - ey[y]) + hcz * fz)
                 qn[g, y, x] = new
                 if t == 0:
@@ -318,18 +339,27 @@
                     acc[3, y, x] += cz * new
             return tuple(carried)
 
-        lax.fori_loop(0, X, body, tuple(start))
-
-    def fold(f, y, dst):
-        @pl.loop(0, X)
-        def _(x):
-            dst[y, pl.ds(XO + x, 1), :] = jnp.sum(acc[f, y, x], axis=0, keepdims=True)
+        lax.fori_loop(0, X, body, tuple(start), unroll=2)
+
+    def fold(fields):
+        @pl.loop(0, X // U)
+        def _(i):
+            at = pl.multiple_of(i * U, U)
+            for f, (dst, first) in enumerate(fields):
+                for y in range(Y):
+                    total = jnp.sum(jnp.swapaxes(acc[f, y, pl.ds(at, U)], 0, 1), axis=0)
+                    dst[first + y, pl.ds(pl.multiple_of(XO + at, U), U), :] = total
 
     for t in range(STEPS):
         psum_finish(t, 1)
         unpack(t, 0, te)
         small_start(1 + t, 2, te, te)
-        acc[...] = jnp.zeros_like(acc)
+        if t == 0:
+            @pl.loop(1, G)
+            def _(g):
+                big_start(0, g)
+        for f in range(4 if t else 1):
+            acc[f] = jnp.zeros_like(acc[f])
         small_finish(1 + t, 2, te, te)
         coefficients()
 
@@ -337,22 +367,15 @@
         def _(g):
             advance(t, g)
             if t + 1 < STEPS:
-                for side in range(4):
-                    @pl.when(has[side])
-                    def _():
-                        big(t + 1, g, side, True).start()
+                big_start(t + 1, g)
 
         if t + 1 < STEPS:
+            fold([(drv, 0)])
             for y in range(Y):
-                fold(0, y, drv)
                 put_plane(t + 1, 0, y, drv[y, XO:XO + X, :])
             psum_start(t + 1, 1)
 
-    for y in range(Y):
-        for f, dst, at in ((1, fxe, y + 2), (2, fye, y + 2), (0, te, y), (3, drv, y)):
-            @pl.loop(0, X)
-            def _(x):
-                dst[at, pl.ds(XO + x, 1), :] = jnp.sum(acc[f, y, x], axis=0, keepdims=True)
+    fold([(te, 0), (fxe, 2), (fye, 2), (drv, 0)])
     small_start(3, 1, fxe, fye)
     small_finish(3, 1, fxe, fye)
     for y in range(Y):
@@ -390,12 +413,14 @@
         temp_out[pl.ds(y, X, stride=Y), :] = value
         cb[y + 2, XO:XO + X, :] = 2.0 * h * value / (2.0 * re[y + 2, XO:XO + X, :] + h)
 
-    @pl.loop(0, X)
-    def _(x):
-        for y in range(Y):
-            a, b = row(ca, y + 2, XO + x), row(cb, y + 2, XO + x)
-            for g in range(G):
-                out[pl.ds(g * U * N + x * Y + y, U, stride=N), :] = a * q2[g, y, x] + b
+    @pl.loop(0, N // U)
+    def _(i):
+        at = [place(i, j) for j in range(U)]
+        a = [row(ca, y + 2, XO + x) for y, x in at]
+        b = [row(cb, y + 2, XO + x) for y, x in at]
+        for g in range(G):
+            block = jnp.stack([a[j] * q2[g, at[j][0], at[j][1]] + b[j] for j in range(U)])
+            out[pl.ds(g * U, U), pl.ds(pl.multiple_of(i * U, U), U), :] = jnp.swapaxes(block, 0, 1)
 
     for side in range(4):
         @pl.when(has[side])
@@ -429,7 +454,7 @@
             v(G, Y, X, U, Z), v(G, Y, X, U, Z), v(G, Y, X, U, Z), v(Y + 4, X + 4, U, Z),
             v(2, 2, G, Y, 2, U, Z), v(2, 2, G, 2, X, U, Z), v(4, Y, X, U, Z), v(N, Z),
             v(Y + 4, XA, Z), v(Y + 4, XA, Z), v(Y + 4, XA, Z), v(Y + 4, XA, Z), v(Y + 4, XA, Z), v(Y + 4, XA, Z),
-            v(Y, X + 8, Z), v(Y, X + 8, Z), v(Y + 1, X, Z), v(Y + 1, X, Z), v(Y, X, Z), v(Y, X, Z), v(Y, X, Z),
+            v(Y, X + 8, Z), v(Y, X + 8, Z), v(Y + 1, X, Z), v(Y + 1, X, Z), v(2, Y, X, Z), v(2, Y, X, Z),
             v(Y + 4, XA, Z), v(Y + 4, XA, Z),
             v(3, NO, 2, R, Z), v(3, NO, 2, R, Z), v(3, NO, 2, R, Z),
             v(4 + SWEEPS, 2, 2, Y, Z), v(4 + SWEEPS, 2, 2, X, Z), v(4 + SWEEPS, 2, 2, Y, Z), v(4 + SWEEPS, 2, 2, X, Z),
@@ -437,12 +462,12 @@
         ]
         updated, temperature = pl.pallas_call(
             functools.partial(kernel, (NO, NX, NY, O, X, Y, Z)),
-            out_shape=(jax.ShapeDtypeStruct((O * N, Z), f32), jax.ShapeDtypeStruct((N, Z), f32)),
+            out_shape=(jax.ShapeDtypeStruct((O, N, Z), f32), jax.ShapeDtypeStruct((N, Z), f32)),
             in_specs=[pl.BlockSpec(memory_space=pltpu.VMEM)] * 3,
             out_specs=[pl.BlockSpec(memory_space=pltpu.VMEM)] * 2,
             scratch_shapes=scratch,
             compiler_params=pltpu.CompilerParams(collective_id=0, has_side_effects=True, vmem_limit_bytes=48 * 2**20),
-        )(speeds, distribution.reshape(O * N, Z), relaxation.reshape(N, Z))
+        )(speeds, distribution.reshape(O, N, Z), relaxation.reshape(N, Z))
         return updated.reshape(O, X, Y, Z), temperature.reshape(X, Y, Z)
 
     return jax.shard_map(

time: 125 us -> 102 us (0.82)
  Pallas kernels: 119 us -> 96.3 us
    pallas_call x1, Pallas kernels: 119 us -> 96.3 us  [local(): pl.pallas_call(functools.partial(kernel, (NO, NX, NY, O, X, Y, Z)), out_s...]
where the time goes in v2:
time: 102 us
  Pallas kernels  96.3 us (94%)
  local copies, waits for them, and re-layouts  4.46 us (4%)
    pallas_call x1, Pallas kernels, local(): pl.pallas_call(functools.partial(kernel, (NO, NX, NY, O, X, Y, Z)), out_s...  96.3 us
    unnamed x6, local copies, waits for them, and re-layouts  4.39 us

profile of v2, /device:TPU:0, one launch (start us, length us, event | category | flops | bytes accessed | tf_op | source)
XLA Modules:
  0.0 101.5 jit_solution(9516338808069748954)
XLA Ops:
  0.7 0.1 broadcast_in_dim.8.speed
  0.8 0.0 copy-start
  0.8 1.6 %copy-done = f32[32,32,4,128]{3,2,1,0:T(4,128)S(1)} copy-done((f32[32,32,4,128]{3,2,1,0:T(4,128)S(1)}, f32[32,32,4,128]{3,2,1,0:T(4,128)}, u32[]{:S(2)}) %copy-start) | copy-done | bytes 2097176
  2.4 0.0 copy-start.1
  2.4 0.8 copy-done.1
  3.2 96.3 %shard_map.41 = (f32[32,128,128]{2,1,0:T(8,128)S(1)}, f32[128,128]{1,0:T(8,128)S(1)}) custom-call(f32[3,4,8,128]{3,2,1,0:T(8,128)S(1)} %broadcast_in_dim.8.speed, f32[32,128,128]{2,1,0:T(8,128)S(1)} %bitcast.6, f32[128,128]{1,0:T(8,128)S(1)} %bitcast.8), custom_call_target="tpu_custom_call" | custom-call | tf_op jit(solution)/shard_map/pallas_call | solution.py:463
  99.6 1.3 %copy.6 = f32[32,32,4,128]{3,2,1,0:T(4,128)} copy(f32[32,32,4,128]{3,2,1,0:T(4,128)S(1)} %bitcast.7) | data formatting | bytes 4194304
  100.9 0.6 copy.7
  (3 shorter events, 0.1 us)
Async XLA Ops:
  0.8 1.6 %copy-start = (f32[32,32,4,128]{3,2,1,0:T(4,128)S(1)}, f32[32,32,4,128]{3,2,1,0:T(4,128)}, u32[]{:S(2)}) copy-start(f32[32,32,4,128]{3,2,1,0:T(4,128)} %param.2) | copy-start | bytes 6291460
  2.4 0.8 copy-start.1

commit v3 on v2

--- a/solution.py
+++ b/solution.py
@@ -40,6 +40,7 @@
     R = N // NO
     U = LANE_GROUP
     XO = 8
+    EARLY = (1, (G + 1) // 2)
     mo, mx, my = lax.axis_index("ord"), lax.axis_index("gx"), lax.axis_index("gy")
     has = (mx > 0, mx < NX - 1, my > 0, my < NY - 1)
     peer = ({"gx": mx - 1}, {"gx": mx + 1}, {"gy": my - 1}, {"gy": my + 1})
@@ -354,10 +355,11 @@
         psum_finish(t, 1)
         unpack(t, 0, te)
         small_start(1 + t, 2, te, te)
-        if t == 0:
-            @pl.loop(1, G)
-            def _(g):
-                big_start(0, g)
+
+        @pl.loop(EARLY[t], G)
+        def _(g):
+            big_start(t, g)
+
         for f in range(4 if t else 1):
             acc[f] = jnp.zeros_like(acc[f])
         small_finish(1 + t, 2, te, te)
@@ -367,7 +369,9 @@
         def _(g):
             advance(t, g)
             if t + 1 < STEPS:
-                big_start(t + 1, g)
+                @pl.when(g < EARLY[t + 1])
+                def _():
+                    big_start(t + 1, g)
 
         if t + 1 < STEPS:
             fold([(drv, 0)])

time: 102 us -> 94.3 us (0.925)
  Pallas kernels: 96.3 us -> 88.9 us
    pallas_call x1, Pallas kernels: 96.3 us -> 88.9 us  [local(): pl.pallas_call(functools.partial(kernel, (NO, NX, NY, O, X, Y, Z)), out_s...]
where the time goes in v3:
time: 94.3 us; the launch traced here: 94.1 us
  Pallas kernels  88.9 us (94%)
  local copies, waits for them, and re-layouts  4.46 us (5%)
    pallas_call x1, Pallas kernels, local(): pl.pallas_call(functools.partial(kernel, (NO, NX, NY, O, X, Y, Z)), out_s...  88.9 us
    unnamed x6, local copies, waits for them, and re-layouts  4.39 us

profile of v3, /device:TPU:0, one launch (start us, length us, event | category | flops | bytes accessed | tf_op | source)
XLA Modules:
  0.0 94.1 jit_solution(4948441618284936876)
XLA Ops:
  0.7 0.1 broadcast_in_dim.8.speed
  0.8 0.0 copy-start
  0.8 1.6 %copy-done = f32[32,32,4,128]{3,2,1,0:T(4,128)S(1)} copy-done((f32[32,32,4,128]{3,2,1,0:T(4,128)S(1)}, f32[32,32,4,128]{3,2,1,0:T(4,128)}, u32[]{:S(2)}) %copy-start) | copy-done | bytes 2097176
  2.4 0.0 copy-start.1
  2.4 0.8 copy-done.1
  3.2 88.9 %shard_map.41 = (f32[32,128,128]{2,1,0:T(8,128)S(1)}, f32[128,128]{1,0:T(8,128)S(1)}) custom-call(f32[3,4,8,128]{3,2,1,0:T(8,128)S(1)} %broadcast_in_dim.8.speed, f32[32,128,128]{2,1,0:T(8,128)S(1)} %bitcast.6, f32[128,128]{1,0:T(8,128)S(1)} %bitcast.8), custom_call_target="tpu_custom_call" | custom-call | tf_op jit(solution)/shard_map/pallas_call | solution.py:467
  92.1 1.3 %copy.6 = f32[32,32,4,128]{3,2,1,0:T(4,128)} copy(f32[32,32,4,128]{3,2,1,0:T(4,128)S(1)} %bitcast.7) | data formatting | bytes 4194304
  93.5 0.6 copy.7
  (3 shorter events, 0.1 us)
Async XLA Ops:
  0.8 1.6 %copy-start = (f32[32,32,4,128]{3,2,1,0:T(4,128)S(1)}, f32[32,32,4,128]{3,2,1,0:T(4,128)}, u32[]{:S(2)}) copy-start(f32[32,32,4,128]{3,2,1,0:T(4,128)} %param.2) | copy-start | bytes 6291460
  2.4 0.8 copy-start.1
